TPU v7x, 32 devices: a whole 2x2x4 slice. The times are simulated.
32 devices in a mesh: dp: 16 (over z, x, core), expert: 2 (over y).
Axes of the slice: x: 2, y: 2, z: 4, core: 2. Of those that a mesh axis runs over, the one named last changes fastest.
Arguments:
- tokens: bfloat16 [2048, 2048], P('dp', 'expert'), may hold values from -6 to 6
- gate_probs: float32 [2048, 6], P('dp'), may hold values from 0.05 to 0.4
- routes: int32 [2048, 6], P('dp'), may hold values from 0 to 15, all different within a row; in each aligned block of 128 rows (0 to 127, 128 to 255, ...) at most 54 rows name the same one
- gate_weight: bfloat16 [16, 1408, 2048], P('dp', 'expert'), may hold values from -0.125 to 0.125
- up_weight: bfloat16 [16, 1408, 2048], P('dp', 'expert'), may hold values from -0.125 to 0.125
- down_weight: bfloat16 [16, 1408, 2048], P('dp', 'expert'), may hold values from -0.15625 to 0.15625
- out_grad: bfloat16 [2048, 2048], P('dp', 'expert'), may hold values from -6 to 6
Outputs:
- layer_out: bfloat16 [2048, 2048], P('dp', 'expert')
- d_tokens: bfloat16 [2048, 2048], P('dp', 'expert')
- gate_grad: float32 [2048, 6], P('dp')
- d_gate_weight: bfloat16 [16, 1408, 2048], P('dp', 'expert')
- d_up_weight: bfloat16 [16, 1408, 2048], P('dp', 'expert')
- d_down_weight: bfloat16 [16, 1408, 2048], P('dp', 'expert')
Inputs may be any that keep to these rules, and one draw needn't show every extreme that they name: `routes`: each row names 6 different experts. In every aligned block of 128 rows no expert is named by more than 54 rows, a bound that some block reaches.
All inputs are finite; a program needn't handle non-finite values.
Results may differ from a plain program's by a relative error of at most 0.0085.
Values may be sent and summed in bfloat16 or wider, within the bound.
No kernel may reach another device: no remote copies, remote signals or barrier semaphores. Data moves between devices by JAX's collectives and lax.ppermute only.
A program may use at most 128 MiB of HBM per device.

v0:
```python
import jax
import jax.numpy as jnp
from jax import lax
from jax.sharding import PartitionSpec as P


def contract_rows(left, right):
    return lax.dot_general(
        left, right, (((0,), (0,)), ((), ())), preferred_element_type=jnp.float32
    )


def contract_last(left, right):
    return lax.dot_general(
        left, right, (((1,), (1,)), ((), ())), preferred_element_type=jnp.float32
    )


def on_device(tokens, gate_probs, routes, gate_weight, up_weight, down_weight, out_grad):
    tok_rows = routes.shape[0]
    top_count = routes.shape[1]
    experts_count = lax.axis_size("dp")
    capacity = tok_rows * top_count * 9 // (8 * experts_count)
    slot_total = experts_count * capacity
    feature_count = gate_weight.shape[2]
    slice_count = tokens.shape[1]
    flat_routes = routes.reshape(-1)
    onehot = (flat_routes[:, None] == jnp.arange(experts_count, dtype=jnp.int32)[None, :]).astype(
        jnp.int32
    )
    earlier = jnp.cumsum(onehot, axis=0) - onehot
    slot_index = jnp.sum(earlier * onehot, axis=1)
    target = flat_routes * capacity + slot_index
    matches = target[None, :] == jnp.arange(slot_total, dtype=jnp.int32)[:, None]
    pair_match = matches.reshape(slot_total, tok_rows, top_count).astype(jnp.float32)
    placing_full = jnp.sum(pair_match, axis=2)
    combine = jnp.sum(pair_match * gate_probs[None, :, :], axis=2)
    slot_gate = jnp.sum(combine, axis=1)
    placing = placing_full.astype(jnp.bfloat16)
    whole_grad = lax.all_gather(out_grad, "expert", axis=1, tiled=True)
    send_x = jnp.dot(placing, tokens, preferred_element_type=jnp.float32).astype(jnp.bfloat16)
    send_g = (
        slot_gate[:, None] * jnp.dot(placing, out_grad, preferred_element_type=jnp.float32)
    ).astype(jnp.bfloat16)
    piece_x, piece_g = (
        lax.all_to_all(
            send_x.reshape(experts_count, capacity, slice_count),
            "dp",
            split_axis=0,
            concat_axis=0,
            tiled=True,
        ),
        lax.all_to_all(
            send_g.reshape(experts_count, capacity, slice_count),
            "dp",
            split_axis=0,
            concat_axis=0,
            tiled=True,
        ),
    )
    recv_x, recv_g = (
        lax.all_gather(piece_x, "expert", axis=2, tiled=True),
        lax.all_gather(piece_g, "expert", axis=2, tiled=True),
    )
    inputs = recv_x.reshape(-1, feature_count)
    grads_in = recv_g.reshape(-1, feature_count)
    w_gate = gate_weight[0]
    w_up = up_weight[0]
    w_down = down_weight[0]
    pre_gate = contract_last(inputs, w_gate)
    pre_up = contract_last(inputs, w_up)
    sigmoid_gate = jax.nn.sigmoid(pre_gate)
    activated = pre_gate * sigmoid_gate
    hidden = (activated * pre_up).astype(jnp.bfloat16)
    part_out = jnp.dot(hidden, w_down, preferred_element_type=jnp.float32).astype(jnp.bfloat16)
    part_out = part_out.reshape(experts_count, capacity, feature_count)
    back_out = lax.all_to_all(part_out, "dp", split_axis=0, concat_axis=0, tiled=True)
    d_hidden = contract_last(grads_in, w_down)
    d_down = contract_rows(hidden, grads_in).astype(jnp.bfloat16)
    d_pre_gate = (
        d_hidden * pre_up * sigmoid_gate * (1.0 + pre_gate * (1.0 - sigmoid_gate))
    ).astype(jnp.bfloat16)
    d_pre_up = (d_hidden * activated).astype(jnp.bfloat16)
    d_gate_w = contract_rows(d_pre_gate, inputs).astype(jnp.bfloat16)
    d_up_w = contract_rows(d_pre_up, inputs).astype(jnp.bfloat16)
    both_pre = jnp.concatenate([d_pre_gate, d_pre_up], axis=1)
    both_weights = jnp.concatenate([w_gate, w_up], axis=0)
    part_grad = jnp.dot(both_pre, both_weights, preferred_element_type=jnp.float32).astype(
        jnp.bfloat16
    )
    part_grad = part_grad.reshape(experts_count, capacity, feature_count)
    back_grad = lax.all_to_all(part_grad, "dp", split_axis=0, concat_axis=0, tiled=True)
    out_flat = back_out.reshape(-1, feature_count)
    grad_flat = back_grad.reshape(-1, feature_count)
    gate_high = combine.astype(jnp.bfloat16)
    gate_low = (combine - gate_high.astype(jnp.float32)).astype(jnp.bfloat16)
    mixed_part = contract_rows(gate_high, out_flat) + contract_rows(gate_low, out_flat)
    grad_part = contract_rows(placing, grad_flat)
    pair_scores = contract_last(out_flat, whole_grad)
    slot_dot = jnp.sum(pair_scores * placing_full, axis=1)
    gate_part = slot_dot[target].reshape(tok_rows, top_count)
    layer_sum, token_sum = (
        lax.psum_scatter(mixed_part, "expert", scatter_dimension=1, tiled=True),
        lax.psum_scatter(grad_part, "expert", scatter_dimension=1, tiled=True),
    )
    gate_grad = lax.psum(gate_part, "expert")
    return (
        layer_sum.astype(jnp.bfloat16),
        token_sum.astype(jnp.bfloat16),
        gate_grad,
        d_gate_w[None],
        d_up_w[None],
        d_down[None],
    )


def solution(mesh):
    return jax.shard_map(
        on_device,
        mesh=mesh,
        in_specs=(
            P("dp", "expert"),
            P("dp", None),
            P("dp", None),
            P("dp", "expert", None),
            P("dp", "expert", None),
            P("dp", "expert", None),
            P("dp", "expert"),
        ),
        out_specs=(
            P("dp", "expert"),
            P("dp", "expert"),
            P("dp", None),
            P("dp", "expert", None),
            P("dp", "expert", None),
            P("dp", "expert", None),
        ),
        check_vma=False,
    )
```

profile of v0, /device:TPU:20, one launch (start us, length us, event | category | flops | bytes accessed | tf_op | source)
XLA Modules:
  0.0 419.8 jit_solution(15894959058864705970)
XLA Ops:
  7.2 0.9 copy.21
  8.2 0.1 eq.43
  8.3 0.1 eq.39
  8.5 1.7 reduce-window.6
  10.2 0.3 slice_reduce_fusion
  10.5 0.1 fusion.23
  10.6 0.1 reduce_sum.50
  10.7 0.6 broadcast_multiply_fusion
  11.4 2.1 select_reduce_fusion
  13.5 2.9 convolution_convert_fusion.4
  16.4 2.6 reshape.105
  19.0 48.2 %all_to_all.20 = bf16[16,54,1024]{2,1,0:T(8,128)(2,1)} all-to-all(bf16[16,54,1024]{2,1,0:T(8,128)(2,1)} %reshape.105), channel_id=1, replica_groups=mesh['dp'=16,'expert'=2] {'dp'}, dimensions={0} | all-to-all | bytes 3538944 | tf_op jit(solution)/shard_map/all_to_all | solution.py:46
  67.4 2.8 multiply_convert_fusion
  70.1 2.6 reshape.109
  72.8 47.1 %all_to_all.21 = bf16[16,54,1024]{2,1,0:T(8,128)(2,1)} all-to-all(bf16[16,54,1024]{2,1,0:T(8,128)(2,1)} %reshape.109), channel_id=1, replica_groups=mesh['dp'=16,'expert'=2] {'dp'}, dimensions={0} | all-to-all | bytes 3538944 | tf_op jit(solution)/shard_map/all_to_all | solution.py:53
  120.0 4.8 %reshape.106 = bf16[864,2048]{1,0:T(8,128)(2,1)} reshape(bf16[16,54,2048]{2,1,0:T(8,128)(2,1)} %all-gather.3.cloned.1.call-done) | data formatting | bytes 7077888 | tf_op jit(solution)/shard_map/reshape | solution.py:65
  124.7 8.2 %fusion.27 = f32[864,704]{0,1:T(8,128)} fusion(bf16[864,2048]{1,0:T(8,128)(2,1)} %reshape.106, bf16[1,704,2048]{2,1,0:T(8,128)(2,1)} %param.11), kind=kOutput, calls=%fused_computation.51 | convolution fusion | flops 2491416576 | bytes 8855552 | tf_op jit(solution)/shard_map/dot_general | solution.py:14
  133.0 36.7 %all-gather.5.cloned.1.call-done = bf16[16,54,2048]{2,1,0:T(8,128)(2,1)} async-done(((bf16[16,54,1024]{2,1,0:T(8,128)(2,1)}), bf16[16,54,2048]{2,1,0:T(8,128)(2,1)}) %all-gather.5.cloned.1.call-update) | async-done | bytes 3538960 | tf_op jit(solution)/shard_map/all_gather | solution.py:63
  169.7 4.7 %reshape.110 = bf16[864,2048]{1,0:T(8,128)(2,1)} reshape(bf16[16,54,2048]{2,1,0:T(8,128)(2,1)} %all-gather.5.cloned.1.call-done) | data formatting | bytes 7077888 | tf_op jit(solution)/shard_map/reshape | solution.py:66
  174.4 5.3 %fusion.10 = f32[864,704]{0,1:T(8,128)S(1)} fusion(bf16[864,2048]{1,0:T(8,128)(2,1)} %reshape.110, bf16[1,704,2048]{2,1,0:T(8,128)(2,1)S(1)} %copy-done), kind=kOutput, calls=%fused_computation.16 | convolution fusion | flops 2491416576 | bytes 8855552 | tf_op jit(solution)/shard_map/dot_general | solution.py:14
  179.8 5.3 %multiply_convert_fusion.2 = (bf16[864,704]{0,1:T(8,128)(2,1)S(1)}, bf16[864,704]{0,1:T(8,128)(2,1)S(1)}, bf16[864,704]{0,1:T(8,128)(2,1)}) fusion(f32[864,704]{0,1:T(8,128)S(1)} %fusion.10, f32[864,704]{0,1:T(8,128)S(1)} %copy-done.12, bf16[864,2048]{1,0:T(8,128)(2,1)S(1)} %copy-done.7, bf16[1,704,2048]{2,1,0:T(8,128)(2,1)S(1)} %copy-done.11), kind=kOutput, calls=%fused_computation.25 | convolution fusion | flops 2500540416 | bytes 14938112 | tf_op jit(solution)/shard_map/dot_general | solution.py:14
  185.1 1.1 copy-done.13
  186.2 0.3 copy-done.15
  186.5 7.3 %fusion.4 = bf16[864,2048]{1,0:T(8,128)(2,1)} fusion(bf16[704,2048]{1,0:T(8,128)(2,1)S(1)} %bitcast.57, bf16[704,2048]{1,0:T(8,128)(2,1)S(1)} %bitcast.58, bf16[864,704]{0,1:T(8,128)(2,1)S(1)} %get-tuple-element.22, bf16[864,704]{0,1:T(8,128)(2,1)S(1)} %get-tuple-element.21), kind=kOutput, calls=%fused_computation.7 | convolution fusion | flops 5001003008 | bytes 11739136 | tf_op jit(solution)/shard_map/dot_general | solution.py:88
  193.8 4.8 %reshape.111 = bf16[16,54,2048]{2,1,0:T(8,128)(2,1)} reshape(bf16[864,2048]{1,0:T(8,128)(2,1)} %fusion.4) | data formatting | bytes 7077888 | tf_op jit(solution)/shard_map/reshape | solution.py:91
  198.6 6.0 %all-to-all-start.3 = ((bf16[16,54,2048]{2,1,0:T(8,128)(2,1)}), bf16[16,54,2048]{2,1,0:T(8,128)(2,1)}, u32[]{:S(2)}, u32[]{:S(2)}) async-start(bf16[16,54,2048]{2,1,0:T(8,128)(2,1)} %reshape.111), calls=%async_computation.4 | async-start | bytes 7340032 | tf_op jit(solution)/shard_map/all_to_all | solution.py:92
  204.6 5.7 %convolution_convert_fusion = bf16[864,2048]{1,0:T(8,128)(2,1)} fusion(bf16[864,704]{0,1:T(8,128)(2,1)} %get-tuple-element.23, bf16[1,704,2048]{2,1,0:T(8,128)(2,1)S(1)} %copy-done), kind=kOutput, calls=%fused_computation.6 | convolution fusion | flops 2493186048 | bytes 7639040 | tf_op jit(solution)/shard_map/dot_general | solution.py:75
  210.4 4.8 %reshape.107 = bf16[16,54,2048]{2,1,0:T(8,128)(2,1)} reshape(bf16[864,2048]{1,0:T(8,128)(2,1)} %convolution_convert_fusion) | data formatting | bytes 7077888 | tf_op jit(solution)/shard_map/reshape | solution.py:76
  215.1 71.0 %all-to-all-done.3 = bf16[16,54,2048]{2,1,0:T(8,128)(2,1)} async-done(((bf16[16,54,2048]{2,1,0:T(8,128)(2,1)}), bf16[16,54,2048]{2,1,0:T(8,128)(2,1)}, u32[]{:S(2)}, u32[]{:S(2)}) %all-to-all-start.3) | async-done | bytes 3538976 | tf_op jit(solution)/shard_map/all_to_all | solution.py:92
  286.1 4.7 %all-to-all-start.1 = ((bf16[16,54,2048]{2,1,0:T(8,128)(2,1)}), bf16[16,54,2048]{2,1,0:T(8,128)(2,1)}, u32[]{:S(2)}, u32[]{:S(2)}) async-start(bf16[16,54,2048]{2,1,0:T(8,128)(2,1)} %reshape.107), calls=%async_computation.1 | async-start | bytes 7340032 | tf_op jit(solution)/shard_map/all_to_all | solution.py:77
  290.8 3.2 reshape.112
  294.0 2.8 fusion.31
  296.9 1.0 mul.78
  297.9 14.7 %all_gather.11 = bf16[128,2048]{1,0:T(8,128)(2,1)} all-gather(bf16[128,1024]{1,0:T(8,128)(2,1)} %param.13), channel_id=1, replica_groups=mesh['dp'=16,'expert'=2] {'expert'}, dimensions={1}, use_global_device_ids=true | all-gather | bytes 786432 | tf_op jit(solution)/shard_map/all_gather | solution.py:40
  312.6 59.7 %all-to-all-done.1 = bf16[16,54,2048]{2,1,0:T(8,128)(2,1)} async-done(((bf16[16,54,2048]{2,1,0:T(8,128)(2,1)}), bf16[16,54,2048]{2,1,0:T(8,128)(2,1)}, u32[]{:S(2)}, u32[]{:S(2)}) %all-to-all-start.1) | async-done | bytes 3538976 | tf_op jit(solution)/shard_map/all_to_all | solution.py:77
  372.2 3.2 reshape.108
  375.5 2.1 fusion.19
  377.6 1.7 convolution_add_fusion
  379.4 7.3 %fusion.9 = bf16[1,704,2048]{2,1,0:T(8,128)(2,1)} fusion(bf16[864,704]{0,1:T(8,128)(2,1)} %get-tuple-element.23, bf16[864,2048]{1,0:T(8,128)(2,1)} %reshape.110), kind=kOutput, calls=%fused_computation.15 | convolution fusion | flops 2492858368 | bytes 7639040 | tf_op jit(solution)/shard_map/dot_general | solution.py:8
  386.6 4.4 %fusion.7 = bf16[1,704,2048]{2,1,0:T(8,128)(2,1)} fusion(bf16[864,704]{0,1:T(8,128)(2,1)S(1)} %copy-done.16, bf16[864,2048]{1,0:T(8,128)(2,1)S(1)} %copy-done.8), kind=kOutput, calls=%fused_computation.13 | convolution fusion | flops 2492858368 | bytes 7639040 | tf_op jit(solution)/shard_map/dot_general | solution.py:8
  391.1 4.4 %fusion.8 = bf16[1,704,2048]{2,1,0:T(8,128)(2,1)} fusion(bf16[864,704]{0,1:T(8,128)(2,1)S(1)} %copy-done.14, bf16[864,2048]{1,0:T(8,128)(2,1)S(1)} %copy-done.8), kind=kOutput, calls=%fused_computation.14 | convolution fusion | flops 2492858368 | bytes 7639040 | tf_op jit(solution)/shard_map/dot_general | solution.py:8
  395.6 1.2 fusion.17
  396.7 3.2 gather_fusion
  399.9 0.1 reshape.113
  400.1 8.9 %psum.7 = f32[128,6]{1,0:T(8,128)S(1)} all-reduce(f32[128,6]{1,0:T(8,128)S(1)} %reshape.113), channel_id=1, replica_groups=mesh['dp'=16,'expert'=2] {'expert'}, use_global_device_ids=true, to_apply=%region_9.10 | all-reduce | flops 768 | bytes 6144 | tf_op jit(solution)/shard_map/psum | solution.py:106
  409.0 0.7 copy.26
  409.7 1.8 convert_element_type.73
  411.4 1.8 convert_element_type.68
  (48 shorter events, 0.4 us)
Async XLA Ops:
  7.2 167.2 %copy-start = (bf16[1,704,2048]{2,1,0:T(8,128)(2,1)S(1)}, bf16[1,704,2048]{2,1,0:T(8,128)(2,1)}, u32[]{:S(2)}) copy-start(bf16[1,704,2048]{2,1,0:T(8,128)(2,1)} %param.12) | copy-start | bytes 8650756
  7.2 112.8 %all-gather.3.cloned.1.call-start = ((), (), s32[]{:S(2)}) async-start(), calls=%async_computation.6 | async-start | bytes 5505024 | tf_op jit(solution)/shard_map/all_gather | solution.py:62
  13.5 53.9 %copy-start.4 = (f32[864,128]{1,0:T(8,128)}, f32[864,128]{1,0:T(8,128)S(1)}, u32[]{:S(2)}) copy-start(f32[864,128]{1,0:T(8,128)S(1)} %get-tuple-element.20) | copy-start | bytes 1327108
  67.3 102.4 %all-gather.5.cloned.1.call-start = ((), (), s32[]{:S(2)}) async-start(), calls=%async_computation.8 | async-start | bytes 5505024 | tf_op jit(solution)/shard_map/all_gather | solution.py:63
  174.4 5.3 %copy-start.7 = (bf16[864,2048]{1,0:T(8,128)(2,1)S(1)}, bf16[864,2048]{1,0:T(8,128)(2,1)}, u32[]{:S(2)}) copy-start(bf16[864,2048]{1,0:T(8,128)(2,1)} %reshape.106) | copy-start | bytes 10616836
  174.4 5.4 %copy-start.11 = (bf16[1,704,2048]{2,1,0:T(8,128)(2,1)S(1)}, bf16[1,704,2048]{2,1,0:T(8,128)(2,1)}, u32[]{:S(2)}) copy-start(bf16[1,704,2048]{2,1,0:T(8,128)(2,1)} %param.10) | copy-start | bytes 8650756
  174.4 5.4 %copy-start.12 = (f32[864,704]{0,1:T(8,128)S(1)}, f32[864,704]{0,1:T(8,128)}, u32[]{:S(2)}) copy-start(f32[864,704]{0,1:T(8,128)} %fusion.27) | copy-start | bytes 7299076
  179.8 6.8 %copy-start.10 = (bf16[1,704,2048]{2,1,0:T(8,128)(2,1)S(1)}, bf16[1,704,2048]{2,1,0:T(8,128)(2,1)}, u32[]{:S(2)}) copy-start(bf16[1,704,2048]{2,1,0:T(8,128)(2,1)} %param.11) | copy-start | bytes 8650756
  185.1 1.1 copy-start.13
  185.1 1.5 copy-start.15
  198.6 87.5 %all-to-all-start.3 = ((bf16[16,54,2048]{2,1,0:T(8,128)(2,1)}), bf16[16,54,2048]{2,1,0:T(8,128)(2,1)}, u32[]{:S(2)}, u32[]{:S(2)}) async-start(bf16[16,54,2048]{2,1,0:T(8,128)(2,1)} %reshape.111), calls=%async_computation.4 | async-start | bytes 7340032 | tf_op jit(solution)/shard_map/all_to_all | solution.py:92
  286.1 86.1 %all-to-all-start.1 = ((bf16[16,54,2048]{2,1,0:T(8,128)(2,1)}), bf16[16,54,2048]{2,1,0:T(8,128)(2,1)}, u32[]{:S(2)}, u32[]{:S(2)}) async-start(bf16[16,54,2048]{2,1,0:T(8,128)(2,1)} %reshape.107), calls=%async_computation.1 | async-start | bytes 7340032 | tf_op jit(solution)/shard_map/all_to_all | solution.py:77
  290.8 118.9 %reduce-scatter.5.cloned.1.call-start = ((), (), s32[]{:S(2)}) async-start(), calls=%async_computation.9 | async-start | bytes 1572864 | tf_op jit(solution)/shard_map/reduce_scatter | solution.py:104
  296.8 114.6 %reduce-scatter.3.cloned.1.call-start = ((), (), s32[]{:S(2)}) async-start(), calls=%async_computation.7 | async-start | bytes 1572864 | tf_op jit(solution)/shard_map/reduce_scatter | solution.py:103
  375.4 3.9 copy-start.2
  375.5 2.1 copy-start.6
  379.4 7.3 %copy-start.8 = (bf16[864,2048]{1,0:T(8,128)(2,1)S(1)}, bf16[864,2048]{1,0:T(8,128)(2,1)}, u32[]{:S(2)}) copy-start(bf16[864,2048]{1,0:T(8,128)(2,1)} %reshape.106) | copy-start | bytes 10616836
  379.4 7.3 %copy-start.16 = (bf16[864,704]{0,1:T(8,128)(2,1)S(1)}, bf16[864,704]{0,1:T(8,128)(2,1)}, u32[]{:S(2)}) copy-start(bf16[864,704]{0,1:T(8,128)(2,1)} %copy-done.15) | copy-start | bytes 3649540
  386.6 4.5 %copy-start.14 = (bf16[864,704]{0,1:T(8,128)(2,1)S(1)}, bf16[864,704]{0,1:T(8,128)(2,1)}, u32[]{:S(2)}) copy-start(bf16[864,704]{0,1:T(8,128)(2,1)} %copy-done.13) | copy-start | bytes 3649540
  391.1 4.5 %copy-start.3 = (bf16[864,2048]{1,0:T(8,128)(2,1)S(1)}, bf16[864,2048]{1,0:T(8,128)(2,1)}, u32[]{:S(2)}) copy-start(bf16[864,2048]{1,0:T(8,128)(2,1)} %copy-done.2) | copy-start | bytes 10616836
  391.1 4.5 %copy-start.5 = (f32[864,128]{1,0:T(8,128)S(1)}, f32[864,128]{1,0:T(8,128)}, u32[]{:S(2)}) copy-start(f32[864,128]{1,0:T(8,128)} %copy-done.4) | copy-start | bytes 1327108
  391.1 4.5 %copy-start.9 = (bf16[128,2048]{1,0:T(8,128)(2,1)S(1)}, bf16[128,2048]{1,0:T(8,128)(2,1)}, u32[]{:S(2)}) copy-start(bf16[128,2048]{1,0:T(8,128)(2,1)} %all_gather.11) | copy-start | bytes 1572868
  395.6 17.7 %copy-start.1 = (bf16[1,704,2048]{2,1,0:T(8,128)(2,1)S(1)}, bf16[1,704,2048]{2,1,0:T(8,128)(2,1)}, u32[]{:S(2)}) copy-start(bf16[1,704,2048]{2,1,0:T(8,128)(2,1)} %param.12) | copy-start | bytes 8650756
Sparse Core Ops, SparseCore 0:
  67.4 49.5 all-gather.2
  120.1 49.5 all-gather.4
  296.9 23.8 reduce-scatter.4
  379.5 18.9 reduce-scatter.2
where the time goes:
time: 421 us; the launch traced here: 420 us
  waiting for transfers between devices  167 us (40%)
  blocking collectives  119 us (28%)
  matrix products  61.5 us (15%)
  local copies, waits for them, and re-layouts  38.8 us (9%)
  between operations  14 us (3%)
  starting transfers between devices  10.9 us (3%)
  other arithmetic  8.15 us (2%)
    all_to_all x1, waiting for transfers between devices, on_device(): lax.all_to_all(part_grad, 'dp', split_axis=0, concat_axis=0, tiled=True)  71 us
    all_to_all x1, waiting for transfers between devices, on_device(): lax.all_to_all(part_out, 'dp', split_axis=0, concat_axis=0, tiled=True)  59.7 us
    all_to_all x1, blocking collectives, on_device(): lax.all_to_all(send_x.reshape(experts_count, capacity, slice_count), 'dp'...  48.2 us
    all_to_all x1, blocking collectives, on_device(): lax.all_to_all(send_g.reshape(experts_count, capacity, slice_count), 'dp'...  47.1 us
    all_gather x1, waiting for transfers between devices, on_device(): lax.all_gather(piece_g, 'expert', axis=2, tiled=True)  36.7 us
    dot_general x6, matrix products, contract_rows(): lax.dot_general(left, right, (((0,), (0,)), ((), ())), preferred_element_...  22.7 us
    dot_general x4, matrix products, contract_last(): lax.dot_general(left, right, (((1,), (1,)), ((), ())), preferred_element_...  20 us
    all_gather x1, blocking collectives, on_device(): whole_grad = lax.all_gather(out_grad, 'expert', axis=1, tiled=True)  14.7 us
  transfers between devices with their start and end apart: 6, of which 3 were waited for; matrix products, arithmetic and copies ran while one was open for 16% of the time, Pallas kernels for 0%

commit v1 on v0

--- a/solution.py
+++ b/solution.py
@@ -1,7 +1,145 @@
+import functools
+
 import jax
 import jax.numpy as jnp
 from jax import lax
+from jax.experimental import pallas as pl
+from jax.experimental.pallas import tpu as pltpu
 from jax.sharding import PartitionSpec as P
+
+QUAD = 4
+
+
+def split3(value):
+    high = value.astype(jnp.bfloat16)
+    rest = value - high.astype(jnp.float32)
+    middle = rest.astype(jnp.bfloat16)
+    low = (rest - middle.astype(jnp.float32)).astype(jnp.bfloat16)
+    return high, middle, low
+
+
+def vmem(count):
+    return [pl.BlockSpec(memory_space=pltpu.VMEM)] * count
+
+
+def params():
+    return pltpu.CompilerParams(vmem_limit_bytes=48 * 1024 * 1024)
+
+
+def prep_kernel(index_ref, routes_ref, probs_ref, tokens_ref, out_ref):
+    rows, width = tokens_ref.shape
+    experts = out_ref.shape[0] - rows
+    me = index_ref[0]
+    routes = routes_ref[...]
+    probs = probs_ref[...]
+    count = index_ref.shape[0] - 1
+    dense = [
+        jnp.sum(jnp.where(routes == (me ^ k), probs, 0.0), axis=0, keepdims=True)
+        for k in range(count)
+    ]
+    per_row = width // rows
+    wide = [
+        jnp.concatenate(dense[k : k + per_row], axis=1) for k in range(0, count, per_row)
+    ]
+    stacked = jnp.concatenate(wide, axis=0)
+    parts = split3(stacked)
+    used = 3 * len(wide)
+    extra = jnp.concatenate(
+        [p.astype(jnp.float32) for p in parts]
+        + [jnp.zeros((experts - used, width), jnp.float32)],
+        axis=0,
+    )
+    out_ref[0:rows, :] = tokens_ref[...]
+    out_ref[rows:, :] = extra.astype(jnp.bfloat16)
+
+
+def one_hot(weights, slots, i, cap, nz):
+    rows = weights.shape[1]
+    total = nz * cap
+    line = lax.broadcasted_iota(jnp.int32, (total, rows), 0).astype(jnp.float32)
+    pieces = []
+    for j in range(nz):
+        k = j * QUAD + i
+        pieces.append(jnp.where(line == slots[k : k + 1, :] + float(j * cap), 1.0, 0.0))
+    return jnp.concatenate(pieces, axis=1)
+
+
+def select_first_kernel(cap, nz, *refs):
+    blocks, outs, w_out, s_out = refs[:nz], refs[nz : nz + QUAD], refs[-2], refs[-1]
+    rows = w_out.shape[1]
+    width = blocks[0].shape[1]
+    count = nz * QUAD
+    per_row = width // rows
+    lines = count // per_row
+    found = []
+    for j in range(nz):
+        extra = blocks[j][rows:, :].astype(jnp.float32)
+        for i in range(QUAD):
+            k = j * QUAD + i
+            at, col = k // per_row, (k % per_row) * rows
+            part = [extra[at + m * lines : at + m * lines + 1, col : col + rows] for m in range(3)]
+            found.append(part[0] + part[1] + part[2])
+    weights = jnp.concatenate(found, axis=0)
+    hit = weights > 0.0
+    tri = jnp.where(
+        lax.broadcasted_iota(jnp.int32, (rows, rows), 0)
+        < lax.broadcasted_iota(jnp.int32, (rows, rows), 1),
+        1.0,
+        0.0,
+    ).astype(jnp.bfloat16)
+    before = jnp.dot(
+        jnp.where(hit, 1.0, 0.0).astype(jnp.bfloat16), tri, preferred_element_type=jnp.float32
+    )
+    slots = jnp.where(hit, before, -1e6)
+    w_out[...] = weights
+    s_out[...] = slots
+    data = jnp.concatenate([b[0:rows, :] for b in blocks], axis=0)
+    for i in range(QUAD):
+        pick = one_hot(weights, slots, i, cap, nz).astype(jnp.bfloat16)
+        outs[i][...] = jnp.dot(pick, data, preferred_element_type=jnp.float32).astype(jnp.bfloat16)
+
+
+def select_scaled_kernel(cap, nz, w_ref, s_ref, *refs):
+    blocks, outs = refs[:nz], refs[nz:]
+    weights, slots = w_ref[...], s_ref[...]
+    data = jnp.concatenate([b[...] for b in blocks], axis=0)
+    for i in range(QUAD):
+        pick = one_hot(weights, slots, i, cap, nz)
+        wide = jnp.concatenate(
+            [weights[j * QUAD + i : j * QUAD + i + 1, :] for j in range(nz)], axis=1
+        )
+        scale = jnp.sum(pick * wide, axis=1, keepdims=True)
+        picked = jnp.dot(pick.astype(jnp.bfloat16), data, preferred_element_type=jnp.float32)
+        outs[i][...] = (scale * picked).astype(jnp.bfloat16)
+
+
+def combine_kernel(cap, nz, weighted, w_ref, s_ref, *refs):
+    pieces, outs = refs[:QUAD], refs[QUAD:]
+    weights, slots = w_ref[...], s_ref[...]
+    rows = weights.shape[1]
+    total = None
+
+    def turned(pick, data):
+        return lax.dot_general(
+            pick, data, (((0,), (0,)), ((), ())), preferred_element_type=jnp.float32
+        )
+
+    for i in range(QUAD):
+        pick = one_hot(weights, slots, i, cap, nz)
+        data = pieces[i][...]
+        if weighted:
+            wide = jnp.concatenate(
+                [weights[j * QUAD + i : j * QUAD + i + 1, :] for j in range(nz)], axis=1
+            )
+            scaled = pick * wide
+            high = scaled.astype(jnp.bfloat16)
+            low = (scaled - high.astype(jnp.float32)).astype(jnp.bfloat16)
+            part = turned(high, data) + turned(low, data)
+        else:
+            part = turned(pick.astype(jnp.bfloat16), data)
+        total = part if total is None else total + part
+    for j in range(nz):
+        outs[j][...] = total[j * rows : (j + 1) * rows, :].astype(jnp.bfloat16)
 
 
 def contract_rows(left, right):
@@ -14,6 +152,132 @@
     return lax.dot_general(
         left, right, (((1,), (1,)), ((), ())), preferred_element_type=jnp.float32
     )
+
+
+def fast(tokens, gate_probs, routes, gate_weight, up_weight, down_weight, out_grad):
+    rows, width = tokens.shape
+    top = routes.shape[1]
+    n_dp = lax.axis_size("dp")
+    nz = n_dp // QUAD
+    cap = rows * top * 9 // (8 * n_dp)
+    slots_q = nz * cap
+    slots_all = n_dp * cap
+    me = lax.axis_index("dp")
+    side = lax.axis_index("expert")
+    hidden_count = gate_weight.shape[1]
+
+    def hop(value, k):
+        return lax.ppermute(value, "dp", [(s, s ^ k) for s in range(n_dp)])
+
+    def swap(value):
+        return lax.ppermute(value, "expert", [(0, 1), (1, 0)])
+
+    bf = functools.partial(jax.ShapeDtypeStruct, dtype=jnp.bfloat16)
+    f32 = functools.partial(jax.ShapeDtypeStruct, dtype=jnp.float32)
+
+    lines = 3 * n_dp * rows // width
+    extra_rows = -(-lines // 8) * 8
+    index = jnp.broadcast_to(me, (n_dp + 1,)).astype(jnp.int32)
+    extended = pl.pallas_call(
+        prep_kernel,
+        out_shape=bf((rows + extra_rows, width)),
+        in_specs=[pl.BlockSpec(memory_space=pltpu.SMEM)] + vmem(3),
+        out_specs=pl.BlockSpec(memory_space=pltpu.VMEM),
+        name="prep",
+    )(index, routes.T, gate_probs.T, tokens)
+    x_blocks = [extended] + [hop(extended, QUAD * j) for j in range(1, nz)]
+    g_blocks = [out_grad] + [hop(out_grad, QUAD * j) for j in range(1, nz)]
+    *x_rows, weights, slots = pl.pallas_call(
+        functools.partial(select_first_kernel, cap, nz),
+        out_shape=[bf((slots_q, width))] * QUAD + [f32((n_dp, rows))] * 2,
+        in_specs=vmem(nz),
+        out_specs=vmem(QUAD + 2),
+        compiler_params=params(),
+        name="select_x",
+    )(*x_blocks)
+    g_rows = pl.pallas_call(
+        functools.partial(select_scaled_kernel, cap, nz),
+        out_shape=[bf((slots_q, width))] * QUAD,
+        in_specs=vmem(nz + 2),
+        out_specs=vmem(QUAD),
+        compiler_params=params(),
+        name="select_g",
+    )(weights, slots, *g_blocks)
+
+    def gather(pieces):
+        mine = [pieces[0]] + [hop(pieces[i], i) for i in range(1, QUAD)]
+        theirs = [swap(piece) for piece in mine]
+        mine, theirs = jnp.concatenate(mine, axis=0), jnp.concatenate(theirs, axis=0)
+        return jnp.concatenate(
+            [jnp.where(side == 0, mine, theirs), jnp.where(side == 0, theirs, mine)], axis=1
+        )
+
+    inputs = gather(x_rows)
+    grads_in = gather(g_rows)
+    w_gate, w_up, w_down = gate_weight[0], up_weight[0], down_weight[0]
+
+    def halves(weight):
+        other = lax.dynamic_slice_in_dim(weight, (1 - side) * width, width, axis=1)
+        own = lax.dynamic_slice_in_dim(weight, side * width, width, axis=1)
+        return other, own
+
+    def give_back(left, weight):
+        other, own = halves(weight)
+        far = jnp.dot(left, other, preferred_element_type=jnp.float32).astype(jnp.bfloat16)
+        near = jnp.dot(left, own, preferred_element_type=jnp.float32)
+        pieces = [None] * QUAD
+        for i in reversed(range(QUAD)):
+            at = slice(i * slots_q, (i + 1) * slots_q)
+            both = (near[at] + swap(far[at]).astype(jnp.float32)).astype(jnp.bfloat16)
+            pieces[i] = both if i == 0 else hop(both, i)
+        return pieces
+
+    def combine(pieces, weighted):
+        blocks = pl.pallas_call(
+            functools.partial(combine_kernel, cap, nz, weighted),
+            out_shape=[bf((rows, width))] * nz,
+            in_specs=vmem(QUAD + 2),
+            out_specs=vmem(nz),
+            compiler_params=params(),
+            name="combine_out" if weighted else "combine_grad",
+        )(weights, slots, *pieces)
+        total = blocks[0].astype(jnp.float32)
+        for j in range(1, nz):
+            total = total + hop(blocks[j], QUAD * j).astype(jnp.float32)
+        return total.astype(jnp.bfloat16)
+
+    pre_gate = contract_last(inputs, w_gate)
+    pre_up = contract_last(inputs, w_up)
+    sigmoid_gate = jax.nn.sigmoid(pre_gate)
+    activated = pre_gate * sigmoid_gate
+    hidden = (activated * pre_up).astype(jnp.bfloat16)
+    layer_out = combine(give_back(hidden, w_down), True)
+
+    d_hidden = contract_last(grads_in, w_down)
+    d_pre_gate = (
+        d_hidden * pre_up * sigmoid_gate * (1.0 + pre_gate * (1.0 - sigmoid_gate))
+    ).astype(jnp.bfloat16)
+    d_pre_up = (d_hidden * activated).astype(jnp.bfloat16)
+    slot_dot = jnp.sum(activated * pre_up * d_hidden, axis=1).reshape(QUAD, slots_q)
+    both_pre = jnp.concatenate([d_pre_gate, d_pre_up], axis=1)
+    both_weights = jnp.concatenate([w_gate, w_up], axis=0)
+    d_tokens = combine(give_back(both_pre, both_weights), False)
+    d_down = contract_rows(hidden, grads_in).astype(jnp.bfloat16)
+    d_gate_w = contract_rows(d_pre_gate, inputs).astype(jnp.bfloat16)
+    d_up_w = contract_rows(d_pre_up, inputs).astype(jnp.bfloat16)
+
+    slot_dot = slot_dot + swap(slot_dot)
+    dots = [slot_dot[0:1]] + [hop(slot_dot[i : i + 1], i) for i in range(1, QUAD)]
+    dots = jnp.concatenate(dots, axis=0).reshape(QUAD, nz, cap).transpose(1, 0, 2)
+    dots = dots.reshape(n_dp, cap)
+    place = jnp.arange(cap, dtype=jnp.float32)[None, :, None] == slots[:, None, :]
+    by_token = jnp.sum(jnp.where(place, dots[:, :, None], 0.0), axis=1)
+    by_token = by_token.reshape(nz, QUAD, rows)
+    scores = [by_token[0]] + [hop(by_token[j], QUAD * j) for j in range(1, nz)]
+    scores = jnp.concatenate(scores, axis=0)
+    named = routes.T[None, :, :] == (me ^ jnp.arange(n_dp, dtype=jnp.int32))[:, None, None]
+    gate_grad = jnp.sum(jnp.where(named, scores[:, None, :], 0.0), axis=0).T / gate_probs
+    return layer_out, d_tokens, gate_grad, d_gate_w[None], d_up_w[None], d_down[None]
 
 
 def on_device(tokens, gate_probs, routes, gate_weight, up_weight, down_weight, out_grad):
@@ -115,8 +379,10 @@
 
 
 def solution(mesh):
+    groups, sides = mesh.shape["dp"], mesh.shape["expert"]
+    step = fast if sides == 2 and groups == 16 else on_device
     return jax.shard_map(
-        on_device,
+        step,
         mesh=mesh,
         in_specs=(
             P("dp", "expert"),

time: 421 us -> 317 us (0.75)
  the two profiles are of different devices: /device:TPU:20 before, /device:TPU:0 now
where the time goes in v1:
time: 317 us; the launch traced here: 314 us
  waiting for transfers between devices  175 us (55%)
  starting transfers between devices  64.6 us (20%)
  matrix products  41.3 us (13%)
  local copies, waits for them, and re-layouts  15.3 us (5%)
  Pallas kernels  8.39 us (3%)
  other arithmetic  7.82 us (2%)
    ppermute x17, waiting for transfers between devices, swap(): return lax.ppermute(value, 'expert', [(0, 1), (1, 0)])  97 us
    ppermute x30, waiting for transfers between devices, hop(): return lax.ppermute(value, 'dp', [(s, s ^ k) for s in range(n_dp)])  78.4 us
    ppermute x30, starting transfers between devices, hop(): return lax.ppermute(value, 'dp', [(s, s ^ k) for s in range(n_dp)])  46.5 us
    ppermute x17, starting transfers between devices, swap(): return lax.ppermute(value, 'expert', [(0, 1), (1, 0)])  18.1 us
    dot_general x3, matrix products, contract_rows(): lax.dot_general(left, right, (((0,), (0,)), ((), ())), preferred_element_...  14.1 us
    dot_general x3, matrix products, contract_last(): lax.dot_general(left, right, (((1,), (1,)), ((), ())), preferred_element_...  11.9 us
    unnamed x68, local copies, waits for them, and re-layouts  11.8 us
    dot_general x2, matrix products, give_back(): near = jnp.dot(left, own, preferred_element_type=jnp.float32)  8.12 us
  transfers between devices with their start and end apart: 47, of which 25 were waited for; matrix products, arithmetic and copies ran while one was open for 10% of the time, Pallas kernels for 2%

profile of v1, /device:TPU:0, one launch (start us, length us, event | category | flops | bytes accessed | tf_op | source)
XLA Modules:
  0.0 313.8 jit_solution(14217540932098484714)
XLA Ops:
  1.2 2.0 prep.1.refs_0_
  3.2 3.0 collective-permute-start
  6.2 2.6 collective-permute-start.1
  9.7 3.5 %collective-permute-start.21 = (bf16[128,1024]{1,0:T(8,128)(2,1)}, bf16[128,1024]{1,0:T(8,128)(2,1)S(1)}, u32[]{:S(2)}, u32[]{:S(2)}) collective-permute-start(bf16[128,1024]{1,0:T(8,128)(2,1)} %refs_0_.1), channel_id=1, source_target_pairs={{0,16},{2,18},{4,20},{6,22},{8,24},{10,26},{12,28},{14,30},{16,0},... | collective-permute-start | bytes 786440 | tf_op jit(solution)/shard_map/ppermute | solution.py:170
  13.2 5.9 %collective-permute-done.refs_1_ = bf16[136,1024]{1,0:T(8,128)(2,1)S(1)} collective-permute-done((bf16[136,1024]{1,0:T(8,128)(2,1)}, bf16[136,1024]{1,0:T(8,128)(2,1)S(1)}, u32[]{:S(2)}, u32[]{:S(2)}) %collective-permute-start) | collective-permute-done | bytes 278560 | tf_op jit(solution)/shard_map/ppermute | solution.py:170
  19.1 4.6 %collective-permute-start.22 = (bf16[128,1024]{1,0:T(8,128)(2,1)}, bf16[128,1024]{1,0:T(8,128)(2,1)S(1)}, u32[]{:S(2)}, u32[]{:S(2)}) collective-permute-start(bf16[128,1024]{1,0:T(8,128)(2,1)} %refs_0_.1), channel_id=1, source_target_pairs={{0,24},{2,26},{4,28},{6,30},{8,16},{10,18},{12,20},{14,22},{16,8},... | collective-permute-start | bytes 786440 | tf_op jit(solution)/shard_map/ppermute | solution.py:170
  23.7 5.2 %collective-permute-done.1.refs_2_ = bf16[136,1024]{1,0:T(8,128)(2,1)S(1)} collective-permute-done((bf16[136,1024]{1,0:T(8,128)(2,1)}, bf16[136,1024]{1,0:T(8,128)(2,1)S(1)}, u32[]{:S(2)}, u32[]{:S(2)}) %collective-permute-start.1) | collective-permute-done | bytes 278560 | tf_op jit(solution)/shard_map/ppermute | solution.py:170
  33.4 18.3 %collective-permute-done.21.refs_2_ = bf16[128,1024]{1,0:T(8,128)(2,1)S(1)} collective-permute-done((bf16[128,1024]{1,0:T(8,128)(2,1)}, bf16[128,1024]{1,0:T(8,128)(2,1)S(1)}, u32[]{:S(2)}, u32[]{:S(2)}) %collective-permute-start.21) | collective-permute-done | bytes 262176 | tf_op jit(solution)/shard_map/ppermute | solution.py:170
  61.4 8.4 %collective-permute-done.26 = bf16[216,1024]{1,0:T(8,128)(2,1)} collective-permute-done((bf16[216,1024]{1,0:T(8,128)(2,1)}, bf16[216,1024]{1,0:T(8,128)(2,1)}, u32[]{:S(2)}, u32[]{:S(2)}) %collective-permute-start.26) | collective-permute-done | bytes 442400 | tf_op jit(solution)/shard_map/ppermute | solution.py:173
  70.9 4.6 %collective-permute-done.6 = bf16[216,1024]{1,0:T(8,128)(2,1)S(1)} collective-permute-done((bf16[216,1024]{1,0:T(8,128)(2,1)S(1)}, bf16[216,1024]{1,0:T(8,128)(2,1)S(1)}, u32[]{:S(2)}, u32[]{:S(2)}) %collective-permute-start.6) | collective-permute-done | bytes 442400 | tf_op jit(solution)/shard_map/ppermute | solution.py:173
  77.1 1.6 collective-permute-start.27
  78.7 1.6 collective-permute-done.25
  82.5 8.1 %collective-permute-done.4 = bf16[216,1024]{1,0:T(8,128)(2,1)S(1)} collective-permute-done((bf16[216,1024]{1,0:T(8,128)(2,1)S(1)}, bf16[216,1024]{1,0:T(8,128)(2,1)S(1)}, u32[]{:S(2)}, u32[]{:S(2)}) %collective-permute-start.4) | collective-permute-done | bytes 442400 | tf_op jit(solution)/shard_map/ppermute | solution.py:170
  92.1 7.2 %collective-permute-done.5 = bf16[216,1024]{1,0:T(8,128)(2,1)S(1)} collective-permute-done((bf16[216,1024]{1,0:T(8,128)(2,1)S(1)}, bf16[216,1024]{1,0:T(8,128)(2,1)S(1)}, u32[]{:S(2)}, u32[]{:S(2)}) %collective-permute-start.5) | collective-permute-done | bytes 442400 | tf_op jit(solution)/shard_map/ppermute | solution.py:170
  101.5 7.7 %collective-permute-done.29 = bf16[216,1024]{1,0:T(8,128)(2,1)S(1)} collective-permute-done((bf16[216,1024]{1,0:T(8,128)(2,1)S(1)}, bf16[216,1024]{1,0:T(8,128)(2,1)S(1)}, u32[]{:S(2)}, u32[]{:S(2)}) %collective-permute-start.29) | collective-permute-done | bytes 442400 | tf_op jit(solution)/shard_map/ppermute | solution.py:173
  109.2 9.4 %collective-permute-done.7 = bf16[216,1024]{1,0:T(8,128)(2,1)S(1)} collective-permute-done((bf16[216,1024]{1,0:T(8,128)(2,1)S(1)}, bf16[216,1024]{1,0:T(8,128)(2,1)S(1)}, u32[]{:S(2)}, u32[]{:S(2)}) %collective-permute-start.7) | collective-permute-done | bytes 442400 | tf_op jit(solution)/shard_map/ppermute | solution.py:173
  118.7 9.4 %collective-permute-done.8 = bf16[216,1024]{1,0:T(8,128)(2,1)S(1)} collective-permute-done((bf16[216,1024]{1,0:T(8,128)(2,1)S(1)}, bf16[216,1024]{1,0:T(8,128)(2,1)S(1)}, u32[]{:S(2)}, u32[]{:S(2)}) %collective-permute-start.8) | collective-permute-done | bytes 442400 | tf_op jit(solution)/shard_map/ppermute | solution.py:173
  128.2 9.1 %collective-permute-done.9 = bf16[216,1024]{1,0:T(8,128)(2,1)S(1)} collective-permute-done((bf16[216,1024]{1,0:T(8,128)(2,1)S(1)}, bf16[216,1024]{1,0:T(8,128)(2,1)S(1)}, u32[]{:S(2)}, u32[]{:S(2)}) %collective-permute-start.9) | collective-permute-done | bytes 442400 | tf_op jit(solution)/shard_map/ppermute | solution.py:173
  137.8 2.2 copy-done.20
  140.1 3.2 %fusion.38 = f32[864,704]{0,1:T(8,128)S(1)} fusion(bf16[1,704,2048]{2,1,0:T(8,128)(2,1)S(1)} %copy-done.20, bf16[864,1024]{1,0:T(8,128)(2,1)S(1)} %get-tuple-element.74, bf16[864,1024]{1,0:T(8,128)(2,1)S(1)} %get-tuple-element.75), kind=kOutput, calls=%fused_computation.87 | convolution fusion | flops 2498494464 | bytes 8855552 | tf_op jit(solution)/shard_map/dot_general | solution.py:152
  143.3 3.2 %fusion.36 = f32[864,704]{0,1:T(8,128)S(1)} fusion(bf16[1,704,2048]{2,1,0:T(8,128)(2,1)S(1)} %copy-done.18, bf16[864,1024]{1,0:T(8,128)(2,1)S(1)} %get-tuple-element.74, bf16[864,1024]{1,0:T(8,128)(2,1)S(1)} %get-tuple-element.75), kind=kOutput, calls=%fused_computation.85 | convolution fusion | flops 2498494464 | bytes 8855552 | tf_op jit(solution)/shard_map/dot_general | solution.py:152
  146.4 5.6 %multiply_reduce_fusion = (f32[864]{0:T(1024)S(1)}, bf16[864,704]{0,1:T(8,128)(2,1)}, bf16[864,704]{0,1:T(8,128)(2,1)S(1)}, bf16[864,704]{0,1:T(8,128)(2,1)S(1)}) fusion(f32[864,704]{0,1:T(8,128)S(1)} %fusion.36, f32[864,704]{0,1:T(8,128)S(1)} %fusion.38, bf16[1,704,2048]{2,1,0:T(8,128)(2,1)S(1)} %copy-done, bf16[864,1024]{1,0:T(8,128)(2,1)S(1)} %get-tuple-element.51, ...), kind=kOutput, calls=%fused_computation.19 | convolution fusion | flops 2508834048 | bytes 14941568 | tf_op jit(solution)/shard_map/dot_general | solution.py:152
  152.0 4.6 %fusion.2 = bf16[1,704,2048]{2,1,0:T(8,128)(2,1)} fusion(bf16[864,704]{0,1:T(8,128)(2,1)S(1)} %get-tuple-element.44, bf16[864,1024]{1,0:T(8,128)(2,1)S(1)} %get-tuple-element.51, bf16[864,1024]{1,0:T(8,128)(2,1)S(1)} %get-tuple-element.50), kind=kOutput, calls=%fused_computation.11 | convolution fusion | flops 2499936256 | bytes 7639040 | tf_op jit(solution)/shard_map/dot_general | solution.py:146
  156.6 4.6 %fusion.1 = bf16[1,704,2048]{2,1,0:T(8,128)(2,1)} fusion(bf16[864,704]{0,1:T(8,128)(2,1)S(1)} %get-tuple-element.45, bf16[864,1024]{1,0:T(8,128)(2,1)S(1)} %get-tuple-element.74, bf16[864,1024]{1,0:T(8,128)(2,1)S(1)} %get-tuple-element.75), kind=kOutput, calls=%fused_computation.10 | convolution fusion | flops 2499936256 | bytes 7639040 | tf_op jit(solution)/shard_map/dot_general | solution.py:146
  162.9 5.7 %fusion.12 = bf16[864,1024]{1,0:T(8,128)(2,1)S(1)} fusion(s32[]{:T(128)S(6)} %select_n.40, bf16[704,2048]{1,0:T(8,128)(2,1)} %bitcast.41, bf16[704,2048]{1,0:T(8,128)(2,1)} %bitcast.39, bf16[864,704]{0,1:T(8,128)(2,1)} %copy-done.26, bf16[864,704]{0,1:T(8,128)(2,1)} %get-tuple-element.43), kind=kOutput, calls=%fused_computation.28 | convolution fusion | flops 2502934528 | bytes 9969668 | tf_op jit(solution)/shard_map/dot_general | solution.py:226
  171.0 4.8 %fusion.7 = f32[864,1024]{1,0:T(8,128)} fusion(s32[]{:T(128)S(6)} %select_n.39, bf16[704,2048]{1,0:T(8,128)(2,1)S(1)} %bitcast.42, bf16[704,2048]{1,0:T(8,128)(2,1)S(1)} %bitcast.40, bf16[864,704]{0,1:T(8,128)(2,1)S(1)} %copy-done.27, bf16[864,704]{0,1:T(8,128)(2,1)S(1)} %copy-done.24), kind=kOutput, calls=%fused_computation.15 | convolution fusion | flops 2502049792 | bytes 11739140 | tf_op jit(solution)/shard_map/dot_general | solution.py:227
  175.8 1.6 convolution_convert_fusion.3
  177.9 3.3 %fusion.16 = f32[864,1024]{1,0:T(8,128)} fusion(bf16[864,704]{0,1:T(8,128)(2,1)S(1)} %copy-done.23, bf16[1,704,2048]{2,1,0:T(8,128)(2,1)S(1)} %copy-done, s32[]{:T(128)S(6)} %select_n.39), kind=kOutput, calls=%fused_computation.31 | convolution fusion | flops 1245708288 | bytes 6242308 | tf_op jit(solution)/shard_map/dot_general | solution.py:227
  189.6 4.9 %collective-permute-done.31 = bf16[216,1024]{1,0:T(8,128)(2,1)} collective-permute-done((bf16[216,1024]{1,0:T(8,128)(2,1)}, bf16[216,1024]{1,0:T(8,128)(2,1)}, u32[]{:S(2)}, u32[]{:S(2)}) %collective-permute-start.31) | collective-permute-done | bytes 442400 | tf_op jit(solution)/shard_map/ppermute | solution.py:173
  195.4 8.6 %collective-permute-done.33 = bf16[216,1024]{1,0:T(8,128)(2,1)} collective-permute-done((bf16[216,1024]{1,0:T(8,128)(2,1)}, bf16[216,1024]{1,0:T(8,128)(2,1)}, u32[]{:S(2)}, u32[]{:S(2)}) %collective-permute-start.33) | collective-permute-done | bytes 442400 | tf_op jit(solution)/shard_map/ppermute | solution.py:173
  204.9 8.6 %collective-permute-done.35 = bf16[216,1024]{1,0:T(8,128)(2,1)} collective-permute-done((bf16[216,1024]{1,0:T(8,128)(2,1)}, bf16[216,1024]{1,0:T(8,128)(2,1)}, u32[]{:S(2)}, u32[]{:S(2)}) %collective-permute-start.35) | collective-permute-done | bytes 442400 | tf_op jit(solution)/shard_map/ppermute | solution.py:173
  213.5 3.0 fusion.20
  216.6 6.4 %collective-permute-done.10 = bf16[216,1024]{1,0:T(8,128)(2,1)} collective-permute-done((bf16[216,1024]{1,0:T(8,128)(2,1)}, bf16[216,1024]{1,0:T(8,128)(2,1)}, u32[]{:S(2)}, u32[]{:S(2)}) %collective-permute-start.10) | collective-permute-done | bytes 442400 | tf_op jit(solution)/shard_map/ppermute | solution.py:173
  223.0 1.7 collective-permute-start.34
  224.7 7.7 %collective-permute-done.11 = bf16[216,1024]{1,0:T(8,128)(2,1)S(1)} collective-permute-done((bf16[216,1024]{1,0:T(8,128)(2,1)}, bf16[216,1024]{1,0:T(8,128)(2,1)S(1)}, u32[]{:S(2)}, u32[]{:S(2)}) %collective-permute-start.11) | collective-permute-done | bytes 442400 | tf_op jit(solution)/shard_map/ppermute | solution.py:173
  232.3 9.5 %collective-permute-done.13 = bf16[216,1024]{1,0:T(8,128)(2,1)S(1)} collective-permute-done((bf16[216,1024]{1,0:T(8,128)(2,1)}, bf16[216,1024]{1,0:T(8,128)(2,1)S(1)}, u32[]{:S(2)}, u32[]{:S(2)}) %collective-permute-start.13) | collective-permute-done | bytes 442400 | tf_op jit(solution)/shard_map/ppermute | solution.py:173
  241.8 6.2 %collective-permute-start.44 = (f32[4,128]{1,0:T(4,128)S(1)}, f32[4,128]{1,0:T(4,128)S(1)}, u32[]{:S(2)}, u32[]{:S(2)}) collective-permute-start(f32[4,128]{1,0:T(4,128)S(1)} %get-tuple-element.69), channel_id=1, source_target_pairs={{0,8},{2,10},{4,12},{6,14},{8,0},{10,2},{12,4},{14,6},{16,24},{18,... | collective-permute-start | bytes 6152 | tf_op jit(solution)/shard_map/ppermute | solution.py:170
  248.0 2.5 collective-permute-done.15
  250.5 7.2 %collective-permute-start.45 = (f32[4,128]{1,0:T(4,128)S(1)}, f32[4,128]{1,0:T(4,128)S(1)}, u32[]{:S(2)}, u32[]{:S(2)}) collective-permute-start(f32[4,128]{1,0:T(4,128)S(1)} %get-tuple-element.68), channel_id=1, source_target_pairs={{0,16},{2,18},{4,20},{6,22},{8,24},{10,26},{12,28},{14,30},{16,0},... | collective-permute-start | bytes 6152 | tf_op jit(solution)/shard_map/ppermute | solution.py:170
  257.7 1.7 fusion.24
  260.9 1.8 collective-permute-start.14
  264.2 4.9 %fusion = bf16[1,704,2048]{2,1,0:T(8,128)(2,1)} fusion(bf16[864,704]{0,1:T(8,128)(2,1)S(1)} %copy-done.25, bf16[864,1024]{1,0:T(8,128)(2,1)S(1)} %copy-done.13, bf16[864,1024]{1,0:T(8,128)(2,1)S(1)} %copy-done.15), kind=kOutput, calls=%fused_computation.9 | convolution fusion | flops 2499936256 | bytes 7639040 | tf_op jit(solution)/shard_map/dot_general | solution.py:146
  269.1 3.0 collective-permute-start.38
  273.9 8.6 %collective-permute-done.16.refs_3_ = bf16[216,1024]{1,0:T(8,128)(2,1)S(1)} collective-permute-done((bf16[216,1024]{1,0:T(8,128)(2,1)S(1)}, bf16[216,1024]{1,0:T(8,128)(2,1)S(1)}, u32[]{:S(2)}, u32[]{:S(2)}) %collective-permute-start.16) | collective-permute-done | bytes 442400 | tf_op jit(solution)/shard_map/ppermute | solution.py:170
  282.5 2.4 combine_out.1
  285.0 3.0 collective-permute-start.18
  291.4 4.1 %collective-permute-done.17 = bf16[128,1024]{1,0:T(8,128)(2,1)S(1)} collective-permute-done((bf16[128,1024]{1,0:T(8,128)(2,1)S(1)}, bf16[128,1024]{1,0:T(8,128)(2,1)S(1)}, u32[]{:S(2)}, u32[]{:S(2)}) %collective-permute-start.17) | collective-permute-done | bytes 262176 | tf_op jit(solution)/shard_map/ppermute | solution.py:170
  295.5 17.5 %collective-permute-done.18 = bf16[128,1024]{1,0:T(8,128)(2,1)S(1)} collective-permute-done((bf16[128,1024]{1,0:T(8,128)(2,1)S(1)}, bf16[128,1024]{1,0:T(8,128)(2,1)S(1)}, u32[]{:S(2)}, u32[]{:S(2)}) %collective-permute-start.18) | collective-permute-done | bytes 262176 | tf_op jit(solution)/shard_map/ppermute | solution.py:170
  (154 shorter events, 48.6 us)
Async XLA Ops:
  0.6 145.8 %copy-start = (bf16[1,704,2048]{2,1,0:T(8,128)(2,1)S(1)}, bf16[1,704,2048]{2,1,0:T(8,128)(2,1)}, u32[]{:S(2)}) copy-start(bf16[1,704,2048]{2,1,0:T(8,128)(2,1)} %param.12) | copy-start | bytes 8650756
  3.2 15.9 %collective-permute-start = (bf16[136,1024]{1,0:T(8,128)(2,1)}, bf16[136,1024]{1,0:T(8,128)(2,1)S(1)}, u32[]{:S(2)}, u32[]{:S(2)}) collective-permute-start(bf16[136,1024]{1,0:T(8,128)(2,1)} %prep.1.refs_0_), channel_id=1, source_target_pairs={{0,8},{2,10},{4,12},{6,14},{8,0},{10,2},{12,4},{14,6},{16,24},{18,... | collective-permute-start | bytes 835592 | tf_op jit(solution)/shard_map/ppermute | solution.py:170
  6.2 22.7 %collective-permute-start.1 = (bf16[136,1024]{1,0:T(8,128)(2,1)}, bf16[136,1024]{1,0:T(8,128)(2,1)S(1)}, u32[]{:S(2)}, u32[]{:S(2)}) collective-permute-start(bf16[136,1024]{1,0:T(8,128)(2,1)} %prep.1.refs_0_), channel_id=1, source_target_pairs={{0,16},{2,18},{4,20},{6,22},{8,24},{10,26},{12,28},{14,30},{16,0},... | collective-permute-start | bytes 835592 | tf_op jit(solution)/shard_map/ppermute | solution.py:170
  8.8 20.1 %collective-permute-start.2 = (bf16[136,1024]{1,0:T(8,128)(2,1)}, bf16[136,1024]{1,0:T(8,128)(2,1)S(1)}, u32[]{:S(2)}, u32[]{:S(2)}) collective-permute-start(bf16[136,1024]{1,0:T(8,128)(2,1)} %prep.1.refs_0_), channel_id=1, source_target_pairs={{0,24},{2,26},{4,28},{6,30},{8,16},{10,18},{12,20},{14,22},{16,8},... | collective-permute-start | bytes 835592 | tf_op jit(solution)/shard_map/ppermute | solution.py:170
  8.8 24.6 %collective-permute-start.20 = (bf16[128,1024]{1,0:T(8,128)(2,1)}, bf16[128,1024]{1,0:T(8,128)(2,1)S(1)}, u32[]{:S(2)}, u32[]{:S(2)}) collective-permute-start(bf16[128,1024]{1,0:T(8,128)(2,1)} %refs_0_.1), channel_id=1, source_target_pairs={{0,8},{2,10},{4,12},{6,14},{8,0},{10,2},{12,4},{14,6},{16,24},{18,... | collective-permute-start | bytes 786440 | tf_op jit(solution)/shard_map/ppermute | solution.py:170
  9.7 42.0 %collective-permute-start.21 = (bf16[128,1024]{1,0:T(8,128)(2,1)}, bf16[128,1024]{1,0:T(8,128)(2,1)S(1)}, u32[]{:S(2)}, u32[]{:S(2)}) collective-permute-start(bf16[128,1024]{1,0:T(8,128)(2,1)} %refs_0_.1), channel_id=1, source_target_pairs={{0,16},{2,18},{4,20},{6,22},{8,24},{10,26},{12,28},{14,30},{16,0},... | collective-permute-start | bytes 786440 | tf_op jit(solution)/shard_map/ppermute | solution.py:170
  19.1 32.6 %collective-permute-start.22 = (bf16[128,1024]{1,0:T(8,128)(2,1)}, bf16[128,1024]{1,0:T(8,128)(2,1)S(1)}, u32[]{:S(2)}, u32[]{:S(2)}) collective-permute-start(bf16[128,1024]{1,0:T(8,128)(2,1)} %refs_0_.1), channel_id=1, source_target_pairs={{0,24},{2,26},{4,28},{6,30},{8,16},{10,18},{12,20},{14,22},{16,8},... | collective-permute-start | bytes 786440 | tf_op jit(solution)/shard_map/ppermute | solution.py:170
  56.4 13.4 %collective-permute-start.26 = (bf16[216,1024]{1,0:T(8,128)(2,1)}, bf16[216,1024]{1,0:T(8,128)(2,1)}, u32[]{:S(2)}, u32[]{:S(2)}) collective-permute-start(bf16[216,1024]{1,0:T(8,128)(2,1)} %get-tuple-element.34), channel_id=1, source_target_pairs={{0,1},{1,0},{2,3},{3,2},{4,5},{5,4},{6,7},{7,6},{8,9},{9,8},{10,11... | collective-permute-start | bytes 1327112 | tf_op jit(solution)/shard_map/ppermute | solution.py:173
  57.9 17.5 %collective-permute-start.6 = (bf16[216,1024]{1,0:T(8,128)(2,1)S(1)}, bf16[216,1024]{1,0:T(8,128)(2,1)S(1)}, u32[]{:S(2)}, u32[]{:S(2)}) collective-permute-start(bf16[216,1024]{1,0:T(8,128)(2,1)S(1)} %get-tuple-element.26), channel_id=1, source_target_pairs={{0,1},{1,0},{2,3},{3,2},{4,5},{5,4},{6,7},{7,6},{8,9},{9,8},{10,11... | collective-permute-start | bytes 1327112 | tf_op jit(solution)/shard_map/ppermute | solution.py:173
  58.4 18.6 %collective-permute-start.23 = (bf16[216,1024]{1,0:T(8,128)(2,1)}, bf16[216,1024]{1,0:T(8,128)(2,1)S(1)}, u32[]{:S(2)}, u32[]{:S(2)}) collective-permute-start(bf16[216,1024]{1,0:T(8,128)(2,1)} %copy-done.10), channel_id=1, source_target_pairs={{0,2},{2,0},{4,6},{6,4},{8,10},{10,8},{12,14},{14,12},{16,18},{18,... | collective-permute-start | bytes 1327112 | tf_op jit(solution)/shard_map/ppermute | solution.py:170
  58.4 18.7 %collective-permute-start.24 = (bf16[216,1024]{1,0:T(8,128)(2,1)}, bf16[216,1024]{1,0:T(8,128)(2,1)S(1)}, u32[]{:S(2)}, u32[]{:S(2)}) collective-permute-start(bf16[216,1024]{1,0:T(8,128)(2,1)} %copy-done.9), channel_id=1, source_target_pairs={{0,4},{2,6},{4,0},{6,2},{8,12},{10,14},{12,8},{14,10},{16,20},{18,... | collective-permute-start | bytes 1327112 | tf_op jit(solution)/shard_map/ppermute | solution.py:170
  59.9 20.4 %collective-permute-start.25 = (bf16[216,1024]{1,0:T(8,128)(2,1)}, bf16[216,1024]{1,0:T(8,128)(2,1)S(1)}, u32[]{:S(2)}, u32[]{:S(2)}) collective-permute-start(bf16[216,1024]{1,0:T(8,128)(2,1)} %copy-done.8), channel_id=1, source_target_pairs={{0,6},{2,4},{4,2},{6,0},{8,14},{10,12},{12,10},{14,8},{16,22},{18,... | collective-permute-start | bytes 1327112 | tf_op jit(solution)/shard_map/ppermute | solution.py:170
  69.8 12.1 %collective-permute-start.3 = (bf16[216,1024]{1,0:T(8,128)(2,1)}, bf16[216,1024]{1,0:T(8,128)(2,1)S(1)}, u32[]{:S(2)}, u32[]{:S(2)}) collective-permute-start(bf16[216,1024]{1,0:T(8,128)(2,1)} %copy-done.7), channel_id=1, source_target_pairs={{0,2},{2,0},{4,6},{6,4},{8,10},{10,8},{12,14},{14,12},{16,18},{18,... | collective-permute-start | bytes 1327112 | tf_op jit(solution)/shard_map/ppermute | solution.py:170
  75.5 15.1 %collective-permute-start.4 = (bf16[216,1024]{1,0:T(8,128)(2,1)S(1)}, bf16[216,1024]{1,0:T(8,128)(2,1)S(1)}, u32[]{:S(2)}, u32[]{:S(2)}) collective-permute-start(bf16[216,1024]{1,0:T(8,128)(2,1)S(1)} %copy-done.6), channel_id=1, source_target_pairs={{0,4},{2,6},{4,0},{6,2},{8,12},{10,14},{12,8},{14,10},{16,20},{18,... | collective-permute-start | bytes 1327112 | tf_op jit(solution)/shard_map/ppermute | solution.py:170
  77.0 22.3 %collective-permute-start.5 = (bf16[216,1024]{1,0:T(8,128)(2,1)S(1)}, bf16[216,1024]{1,0:T(8,128)(2,1)S(1)}, u32[]{:S(2)}, u32[]{:S(2)}) collective-permute-start(bf16[216,1024]{1,0:T(8,128)(2,1)S(1)} %copy-done.4), channel_id=1, source_target_pairs={{0,6},{2,4},{4,2},{6,0},{8,14},{10,12},{12,10},{14,8},{16,22},{18,... | collective-permute-start | bytes 1327112 | tf_op jit(solution)/shard_map/ppermute | solution.py:170
  77.1 23.7 %collective-permute-start.27 = (bf16[216,1024]{1,0:T(8,128)(2,1)S(1)}, bf16[216,1024]{1,0:T(8,128)(2,1)S(1)}, u32[]{:S(2)}, u32[]{:S(2)}) collective-permute-start(bf16[216,1024]{1,0:T(8,128)(2,1)S(1)} %collective-permute-done.23), channel_id=1, source_target_pairs={{0,1},{1,0},{2,3},{3,2},{4,5},{5,4},{6,7},{7,6},{8,9},{9,8},{10,11... | collective-permute-start | bytes 1327112 | tf_op jit(solution)/shard_map/ppermute | solution.py:173
  80.3 21.1 %collective-permute-start.28 = (bf16[216,1024]{1,0:T(8,128)(2,1)S(1)}, bf16[216,1024]{1,0:T(8,128)(2,1)S(1)}, u32[]{:S(2)}, u32[]{:S(2)}) collective-permute-start(bf16[216,1024]{1,0:T(8,128)(2,1)S(1)} %collective-permute-done.24), channel_id=1, source_target_pairs={{0,1},{1,0},{2,3},{3,2},{4,5},{5,4},{6,7},{7,6},{8,9},{9,8},{10,11... | collective-permute-start | bytes 1327112 | tf_op jit(solution)/shard_map/ppermute | solution.py:173
  81.9 27.3 %collective-permute-start.29 = (bf16[216,1024]{1,0:T(8,128)(2,1)S(1)}, bf16[216,1024]{1,0:T(8,128)(2,1)S(1)}, u32[]{:S(2)}, u32[]{:S(2)}) collective-permute-start(bf16[216,1024]{1,0:T(8,128)(2,1)S(1)} %collective-permute-done.25), channel_id=1, source_target_pairs={{0,1},{1,0},{2,3},{3,2},{4,5},{5,4},{6,7},{7,6},{8,9},{9,8},{10,11... | collective-permute-start | bytes 1327112 | tf_op jit(solution)/shard_map/ppermute | solution.py:173
  90.6 28.1 %collective-permute-start.7 = (bf16[216,1024]{1,0:T(8,128)(2,1)S(1)}, bf16[216,1024]{1,0:T(8,128)(2,1)S(1)}, u32[]{:S(2)}, u32[]{:S(2)}) collective-permute-start(bf16[216,1024]{1,0:T(8,128)(2,1)S(1)} %collective-permute-done.3), channel_id=1, source_target_pairs={{0,1},{1,0},{2,3},{3,2},{4,5},{5,4},{6,7},{7,6},{8,9},{9,8},{10,11... | collective-permute-start | bytes 1327112 | tf_op jit(solution)/shard_map/ppermute | solution.py:173
  99.3 28.9 %collective-permute-start.8 = (bf16[216,1024]{1,0:T(8,128)(2,1)S(1)}, bf16[216,1024]{1,0:T(8,128)(2,1)S(1)}, u32[]{:S(2)}, u32[]{:S(2)}) collective-permute-start(bf16[216,1024]{1,0:T(8,128)(2,1)S(1)} %collective-permute-done.4), channel_id=1, source_target_pairs={{0,1},{1,0},{2,3},{3,2},{4,5},{5,4},{6,7},{7,6},{8,9},{9,8},{10,11... | collective-permute-start | bytes 1327112 | tf_op jit(solution)/shard_map/ppermute | solution.py:173
  100.8 36.5 %collective-permute-start.9 = (bf16[216,1024]{1,0:T(8,128)(2,1)S(1)}, bf16[216,1024]{1,0:T(8,128)(2,1)S(1)}, u32[]{:S(2)}, u32[]{:S(2)}) collective-permute-start(bf16[216,1024]{1,0:T(8,128)(2,1)S(1)} %collective-permute-done.5), channel_id=1, source_target_pairs={{0,1},{1,0},{2,3},{3,2},{4,5},{5,4},{6,7},{7,6},{8,9},{9,8},{10,11... | collective-permute-start | bytes 1327112 | tf_op jit(solution)/shard_map/ppermute | solution.py:173
  161.3 16.0 %collective-permute-start.40 = (f32[4,216]{1,0:T(4,128)S(1)}, f32[4,216]{1,0:T(4,128)S(1)}, u32[]{:S(2)}, u32[]{:S(2)}) collective-permute-start(f32[4,216]{1,0:T(4,128)S(1)} %reshape.37), channel_id=1, source_target_pairs={{0,1},{1,0},{2,3},{3,2},{4,5},{5,4},{6,7},{7,6},{8,9},{9,8},{10,11... | collective-permute-start | bytes 10376 | tf_op jit(solution)/shard_map/ppermute | solution.py:173
  169.8 18.6 %collective-permute-start.30 = (bf16[216,1024]{1,0:T(8,128)(2,1)}, bf16[216,1024]{1,0:T(8,128)(2,1)S(1)}, u32[]{:S(2)}, u32[]{:S(2)}) collective-permute-start(bf16[216,1024]{1,0:T(8,128)(2,1)} %get-tuple-element.61), channel_id=1, source_target_pairs={{0,1},{1,0},{2,3},{3,2},{4,5},{5,4},{6,7},{7,6},{8,9},{9,8},{10,11... | collective-permute-start | bytes 1327112 | tf_op jit(solution)/shard_map/ppermute | solution.py:173
  177.4 5.9 %collective-permute-start.41 = (f32[1,216]{1,0:T(1,128)S(1)}, f32[1,216]{1,0:T(1,128)S(1)}, u32[]{:S(2)}, u32[]{:S(2)}) collective-permute-start(f32[1,216]{1,0:T(1,128)S(1)} %get-tuple-element.73), channel_id=1, source_target_pairs={{0,2},{2,0},{4,6},{6,4},{8,10},{10,8},{12,14},{14,12},{16,18},{18,... | collective-permute-start | bytes 2600 | tf_op jit(solution)/shard_map/ppermute | solution.py:170
  177.5 6.7 %collective-permute-start.42 = (f32[1,216]{1,0:T(1,128)S(1)}, f32[1,216]{1,0:T(1,128)S(1)}, u32[]{:S(2)}, u32[]{:S(2)}) collective-permute-start(f32[1,216]{1,0:T(1,128)S(1)} %get-tuple-element.72), channel_id=1, source_target_pairs={{0,4},{2,6},{4,0},{6,2},{8,12},{10,14},{12,8},{14,10},{16,20},{18,... | collective-permute-start | bytes 2600 | tf_op jit(solution)/shard_map/ppermute | solution.py:170
  181.2 13.3 %collective-permute-start.31 = (bf16[216,1024]{1,0:T(8,128)(2,1)}, bf16[216,1024]{1,0:T(8,128)(2,1)}, u32[]{:S(2)}, u32[]{:S(2)}) collective-permute-start(bf16[216,1024]{1,0:T(8,128)(2,1)} %get-tuple-element.60), channel_id=1, source_target_pairs={{0,1},{1,0},{2,3},{3,2},{4,5},{5,4},{6,7},{7,6},{8,9},{9,8},{10,11... | collective-permute-start | bytes 1327112 | tf_op jit(solution)/shard_map/ppermute | solution.py:173
  182.1 21.9 %collective-permute-start.33 = (bf16[216,1024]{1,0:T(8,128)(2,1)}, bf16[216,1024]{1,0:T(8,128)(2,1)}, u32[]{:S(2)}, u32[]{:S(2)}) collective-permute-start(bf16[216,1024]{1,0:T(8,128)(2,1)} %get-tuple-element.59), channel_id=1, source_target_pairs={{0,1},{1,0},{2,3},{3,2},{4,5},{5,4},{6,7},{7,6},{8,9},{9,8},{10,11... | collective-permute-start | bytes 1327112 | tf_op jit(solution)/shard_map/ppermute | solution.py:173
  183.2 30.3 %collective-permute-start.35 = (bf16[216,1024]{1,0:T(8,128)(2,1)}, bf16[216,1024]{1,0:T(8,128)(2,1)}, u32[]{:S(2)}, u32[]{:S(2)}) collective-permute-start(bf16[216,1024]{1,0:T(8,128)(2,1)} %get-tuple-element.58), channel_id=1, source_target_pairs={{0,1},{1,0},{2,3},{3,2},{4,5},{5,4},{6,7},{7,6},{8,9},{9,8},{10,11... | collective-permute-start | bytes 1327112 | tf_op jit(solution)/shard_map/ppermute | solution.py:173
  184.1 3.0 collective-permute-start.43
  187.1 35.9 %collective-permute-start.10 = (bf16[216,1024]{1,0:T(8,128)(2,1)}, bf16[216,1024]{1,0:T(8,128)(2,1)}, u32[]{:S(2)}, u32[]{:S(2)}) collective-permute-start(bf16[216,1024]{1,0:T(8,128)(2,1)} %get-tuple-element.65), channel_id=1, source_target_pairs={{0,1},{1,0},{2,3},{3,2},{4,5},{5,4},{6,7},{7,6},{8,9},{9,8},{10,11... | collective-permute-start | bytes 1327112 | tf_op jit(solution)/shard_map/ppermute | solution.py:173
  188.5 43.9 %collective-permute-start.11 = (bf16[216,1024]{1,0:T(8,128)(2,1)}, bf16[216,1024]{1,0:T(8,128)(2,1)S(1)}, u32[]{:S(2)}, u32[]{:S(2)}) collective-permute-start(bf16[216,1024]{1,0:T(8,128)(2,1)} %get-tuple-element.64), channel_id=1, source_target_pairs={{0,1},{1,0},{2,3},{3,2},{4,5},{5,4},{6,7},{7,6},{8,9},{9,8},{10,11... | collective-permute-start | bytes 1327112 | tf_op jit(solution)/shard_map/ppermute | solution.py:173
  194.5 47.3 %collective-permute-start.13 = (bf16[216,1024]{1,0:T(8,128)(2,1)}, bf16[216,1024]{1,0:T(8,128)(2,1)S(1)}, u32[]{:S(2)}, u32[]{:S(2)}) collective-permute-start(bf16[216,1024]{1,0:T(8,128)(2,1)} %get-tuple-element.63), channel_id=1, source_target_pairs={{0,1},{1,0},{2,3},{3,2},{4,5},{5,4},{6,7},{7,6},{8,9},{9,8},{10,11... | collective-permute-start | bytes 1327112 | tf_op jit(solution)/shard_map/ppermute | solution.py:173
  204.0 46.5 %collective-permute-start.15 = (bf16[216,1024]{1,0:T(8,128)(2,1)}, bf16[216,1024]{1,0:T(8,128)(2,1)S(1)}, u32[]{:S(2)}, u32[]{:S(2)}) collective-permute-start(bf16[216,1024]{1,0:T(8,128)(2,1)} %get-tuple-element.62), channel_id=1, source_target_pairs={{0,1},{1,0},{2,3},{3,2},{4,5},{5,4},{6,7},{7,6},{8,9},{9,8},{10,11... | collective-permute-start | bytes 1327112 | tf_op jit(solution)/shard_map/ppermute | solution.py:173
  216.5 43.0 %collective-permute-start.32 = (bf16[216,1024]{1,0:T(8,128)(2,1)S(1)}, bf16[216,1024]{1,0:T(8,128)(2,1)S(1)}, u32[]{:S(2)}, u32[]{:S(2)}) collective-permute-start(bf16[216,1024]{1,0:T(8,128)(2,1)S(1)} %get-tuple-element.48), channel_id=1, source_target_pairs={{0,2},{2,0},{4,6},{6,4},{8,10},{10,8},{12,14},{14,12},{16,18},{18,... | collective-permute-start | bytes 1327112 | tf_op jit(solution)/shard_map/ppermute | solution.py:170
  223.0 37.9 %collective-permute-start.34 = (bf16[216,1024]{1,0:T(8,128)(2,1)S(1)}, bf16[216,1024]{1,0:T(8,128)(2,1)S(1)}, u32[]{:S(2)}, u32[]{:S(2)}) collective-permute-start(bf16[216,1024]{1,0:T(8,128)(2,1)S(1)} %get-tuple-element.47), channel_id=1, source_target_pairs={{0,4},{2,6},{4,0},{6,2},{8,12},{10,14},{12,8},{14,10},{16,20},{18,... | collective-permute-start | bytes 1327112 | tf_op jit(solution)/shard_map/ppermute | solution.py:170
  232.3 28.6 %collective-permute-start.36 = (bf16[216,1024]{1,0:T(8,128)(2,1)S(1)}, bf16[216,1024]{1,0:T(8,128)(2,1)S(1)}, u32[]{:S(2)}, u32[]{:S(2)}) collective-permute-start(bf16[216,1024]{1,0:T(8,128)(2,1)S(1)} %get-tuple-element.46), channel_id=1, source_target_pairs={{0,6},{2,4},{4,2},{6,0},{8,14},{10,12},{12,10},{14,8},{16,22},{18,... | collective-permute-start | bytes 1327112 | tf_op jit(solution)/shard_map/ppermute | solution.py:170
  241.8 22.1 %collective-permute-start.44 = (f32[4,128]{1,0:T(4,128)S(1)}, f32[4,128]{1,0:T(4,128)S(1)}, u32[]{:S(2)}, u32[]{:S(2)}) collective-permute-start(f32[4,128]{1,0:T(4,128)S(1)} %get-tuple-element.69), channel_id=1, source_target_pairs={{0,8},{2,10},{4,12},{6,14},{8,0},{10,2},{12,4},{14,6},{16,24},{18,... | collective-permute-start | bytes 6152 | tf_op jit(solution)/shard_map/ppermute | solution.py:170
  250.5 13.6 %collective-permute-start.45 = (f32[4,128]{1,0:T(4,128)S(1)}, f32[4,128]{1,0:T(4,128)S(1)}, u32[]{:S(2)}, u32[]{:S(2)}) collective-permute-start(f32[4,128]{1,0:T(4,128)S(1)} %get-tuple-element.68), channel_id=1, source_target_pairs={{0,16},{2,18},{4,20},{6,22},{8,24},{10,26},{12,28},{14,30},{16,0},... | collective-permute-start | bytes 6152 | tf_op jit(solution)/shard_map/ppermute | solution.py:170
  259.4 9.7 %collective-permute-start.46 = (f32[4,128]{1,0:T(4,128)S(1)}, f32[4,128]{1,0:T(4,128)S(1)}, u32[]{:S(2)}, u32[]{:S(2)}) collective-permute-start(f32[4,128]{1,0:T(4,128)S(1)} %get-tuple-element.67), channel_id=1, source_target_pairs={{0,24},{2,26},{4,28},{6,30},{8,16},{10,18},{12,20},{14,22},{16,8},... | collective-permute-start | bytes 6152 | tf_op jit(solution)/shard_map/ppermute | solution.py:170
  260.9 11.3 %collective-permute-start.12 = (bf16[216,1024]{1,0:T(8,128)(2,1)S(1)}, bf16[216,1024]{1,0:T(8,128)(2,1)S(1)}, u32[]{:S(2)}, u32[]{:S(2)}) collective-permute-start(bf16[216,1024]{1,0:T(8,128)(2,1)S(1)} %get-tuple-element.54), channel_id=1, source_target_pairs={{0,2},{2,0},{4,6},{6,4},{8,10},{10,8},{12,14},{14,12},{16,18},{18,... | collective-permute-start | bytes 1327112 | tf_op jit(solution)/shard_map/ppermute | solution.py:170
  260.9 13.0 %collective-permute-start.14 = (bf16[216,1024]{1,0:T(8,128)(2,1)S(1)}, bf16[216,1024]{1,0:T(8,128)(2,1)S(1)}, u32[]{:S(2)}, u32[]{:S(2)}) collective-permute-start(bf16[216,1024]{1,0:T(8,128)(2,1)S(1)} %get-tuple-element.53), channel_id=1, source_target_pairs={{0,4},{2,6},{4,0},{6,2},{8,12},{10,14},{12,8},{14,10},{16,20},{18,... | collective-permute-start | bytes 1327112 | tf_op jit(solution)/shard_map/ppermute | solution.py:170
  264.0 18.5 %collective-permute-start.16 = (bf16[216,1024]{1,0:T(8,128)(2,1)S(1)}, bf16[216,1024]{1,0:T(8,128)(2,1)S(1)}, u32[]{:S(2)}, u32[]{:S(2)}) collective-permute-start(bf16[216,1024]{1,0:T(8,128)(2,1)S(1)} %get-tuple-element.52), channel_id=1, source_target_pairs={{0,6},{2,4},{4,2},{6,0},{8,14},{10,12},{12,10},{14,8},{16,22},{18,... | collective-permute-start | bytes 1327112 | tf_op jit(solution)/shard_map/ppermute | solution.py:170
  264.1 23.8 %collective-permute-start.37 = (bf16[128,1024]{1,0:T(8,128)(2,1)S(1)}, bf16[128,1024]{1,0:T(8,128)(2,1)S(1)}, u32[]{:S(2)}, u32[]{:S(2)}) collective-permute-start(bf16[128,1024]{1,0:T(8,128)(2,1)S(1)} %get-tuple-element.39), channel_id=1, source_target_pairs={{0,8},{2,10},{4,12},{6,14},{8,0},{10,2},{12,4},{14,6},{16,24},{18,... | collective-permute-start | bytes 786440 | tf_op jit(solution)/shard_map/ppermute | solution.py:170
  269.1 21.4 %collective-permute-start.38 = (bf16[128,1024]{1,0:T(8,128)(2,1)S(1)}, bf16[128,1024]{1,0:T(8,128)(2,1)S(1)}, u32[]{:S(2)}, u32[]{:S(2)}) collective-permute-start(bf16[128,1024]{1,0:T(8,128)(2,1)S(1)} %get-tuple-element.40), channel_id=1, source_target_pairs={{0,16},{2,18},{4,20},{6,22},{8,24},{10,26},{12,28},{14,30},{16,0},... | collective-permute-start | bytes 786440 | tf_op jit(solution)/shard_map/ppermute | solution.py:170
  272.2 18.3 %collective-permute-start.39 = (bf16[128,1024]{1,0:T(8,128)(2,1)S(1)}, bf16[128,1024]{1,0:T(8,128)(2,1)S(1)}, u32[]{:S(2)}, u32[]{:S(2)}) collective-permute-start(bf16[128,1024]{1,0:T(8,128)(2,1)S(1)} %get-tuple-element.41), channel_id=1, source_target_pairs={{0,24},{2,26},{4,28},{6,30},{8,16},{10,18},{12,20},{14,22},{16,8},... | collective-permute-start | bytes 786440 | tf_op jit(solution)/shard_map/ppermute | solution.py:170
  284.9 10.6 %collective-permute-start.17 = (bf16[128,1024]{1,0:T(8,128)(2,1)S(1)}, bf16[128,1024]{1,0:T(8,128)(2,1)S(1)}, u32[]{:S(2)}, u32[]{:S(2)}) collective-permute-start(bf16[128,1024]{1,0:T(8,128)(2,1)S(1)} %get-tuple-element.31), channel_id=1, source_target_pairs={{0,8},{2,10},{4,12},{6,14},{8,0},{10,2},{12,4},{14,6},{16,24},{18,... | collective-permute-start | bytes 786440 | tf_op jit(solution)/shard_map/ppermute | solution.py:170
  285.0 28.0 %collective-permute-start.18 = (bf16[128,1024]{1,0:T(8,128)(2,1)S(1)}, bf16[128,1024]{1,0:T(8,128)(2,1)S(1)}, u32[]{:S(2)}, u32[]{:S(2)}) collective-permute-start(bf16[128,1024]{1,0:T(8,128)(2,1)S(1)} %get-tuple-element.32), channel_id=1, source_target_pairs={{0,16},{2,18},{4,20},{6,22},{8,24},{10,26},{12,28},{14,30},{16,0},... | collective-permute-start | bytes 786440 | tf_op jit(solution)/shard_map/ppermute | solution.py:170
  288.0 25.0 %collective-permute-start.19 = (bf16[128,1024]{1,0:T(8,128)(2,1)S(1)}, bf16[128,1024]{1,0:T(8,128)(2,1)S(1)}, u32[]{:S(2)}, u32[]{:S(2)}) collective-permute-start(bf16[128,1024]{1,0:T(8,128)(2,1)S(1)} %get-tuple-element.33), channel_id=1, source_target_pairs={{0,24},{2,26},{4,28},{6,30},{8,16},{10,18},{12,20},{14,22},{16,8},... | collective-permute-start | bytes 786440 | tf_op jit(solution)/shard_map/ppermute | solution.py:170
  (27 other events, 256.0 us)
